TPU v7x, 256 devices: a whole 4x4x8 slice. The times are simulated.
256 devices in a mesh: gx: 32 (over y, x, core), gz: 8 (over z).
Axes of the slice: x: 4, y: 4, z: 8, core: 2. Of those that a mesh axis runs over, the one named last changes fastest.
Arguments:
- velocity: float32 [64, 3, 128, 64, 256], P(None, None, 'gx', 'gz'), may hold values from -40 to 40
- scaled_modes: float32 [64, 128, 64, 256], P(None, 'gx', 'gz'), may hold values from -70 to 70
Outputs:
- orthonormal: float32 [128, 128, 64, 256], P(None, 'gx', 'gz')
- triangle: float32 [128, 128], replicated
- lower_one: float32 [128, 128], replicated
All inputs are finite; a program needn't handle non-finite values.
Results may differ from a plain program's by a relative error of at most 0.0003.
Values sent between devices are 32-bit elements; how exact they have to be, the bound alone decides.
No kernel may reach another device: no remote copies, remote signals or barrier semaphores. Data moves between devices by JAX's collectives and lax.ppermute only.
A program may use at most 128 MiB of HBM per device.

v0:
```python
import jax
import jax.numpy as jnp
from jax import lax
from jax.sharding import PartitionSpec as P

precise = lax.Precision.HIGHEST


def with_halo(block, sides, width):
    for axis, dim in sides:
        count = lax.axis_size(axis)
        forward = [(i, i + 1) for i in range(count - 1)]
        forward.append((count - 1, 0))
        backward = [(target, source) for source, target in forward]
        low = lax.ppermute(
            lax.slice_in_dim(block, block.shape[dim] - width, None, axis=dim), axis, forward
        )
        high = lax.ppermute(lax.slice_in_dim(block, 0, width, axis=dim), axis, backward)
        block = jnp.concatenate([low, block, high], axis=dim)
    return block


def along_wall(field):
    inner = (field[..., 2:] - field[..., :-2]) * 0.5
    bottom = (-3.0 * field[..., 0:1] + 4.0 * field[..., 1:2] - field[..., 2:3]) * 0.5
    top_side = (3.0 * field[..., -1:] - 4.0 * field[..., -2:-1] + field[..., -3:-2]) * 0.5
    return jnp.concatenate([bottom, inner, top_side], -1)


def product(left, right):
    return lax.dot_general(left, right, (((1,), (1,)), ((), ())), precision=precise)


def shards(velocity, scaled_modes):
    snapshots, _, cells_x, cells_z, cells_y = velocity.shape
    columns_old = scaled_modes.shape[0]
    total_cells = cells_x * lax.axis_size("gx") * cells_z * lax.axis_size("gz") * cells_y
    mode_fields = scaled_modes.reshape(columns_old, -1)
    padded = with_halo(velocity, (("gx", 2), ("gz", 3)), 1)
    grad_x = (padded[:, :, 2:, 1:-1] - padded[:, :, :-2, 1:-1]) * 0.5
    grad_z = (padded[:, :, 1:-1, 2:] - padded[:, :, 1:-1, :-2]) * 0.5
    grad_y = along_wall(velocity)
    diagonal_part = (
        grad_x[:, 0] * grad_x[:, 0] + grad_z[:, 1] * grad_z[:, 1] + grad_y[:, 2] * grad_y[:, 2]
    )
    cross_part = (
        grad_z[:, 0] * grad_x[:, 1] + grad_y[:, 0] * grad_x[:, 2] + grad_y[:, 1] * grad_z[:, 2]
    )
    new_fields = (-0.5 * diagonal_part - cross_part).reshape(snapshots, -1)
    stacked = jnp.concatenate([mode_fields, new_fields], 0)
    gram_sum = lax.psum(product(stacked, stacked), ("gx", "gz"))
    lower_one = jnp.linalg.cholesky(gram_sum / total_cells)
    first_pass = lax.linalg.triangular_solve(lower_one, stacked, left_side=True, lower=True)
    second_sum = lax.psum(product(first_pass, first_pass), ("gx", "gz"))
    lower_two = jnp.linalg.cholesky(second_sum / total_cells)
    basis = lax.linalg.triangular_solve(lower_two, first_pass, left_side=True, lower=True)
    triangle = jnp.dot(lower_two.T, lower_one.T, precision=precise)
    return (basis.reshape(stacked.shape[0], cells_x, cells_z, cells_y), triangle, lower_one)


def solution(mesh):
    in_specs = (P(None, None, "gx", "gz", None), P(None, "gx", "gz", None))
    out_specs = (P(None, "gx", "gz", None), P(), P())
    return jax.shard_map(shards, mesh=mesh, in_specs=in_specs, out_specs=out_specs, check_vma=False)
```

profile of v0, /device:TPU:1, one launch (start us, length us, event | category | flops | bytes accessed | tf_op | source)
XLA Modules:
  0.0 683.3 jit_solution(10335882637036311948)
XLA Ops:
  7.2 6.4 copy.45
  13.7 2.7 copy-done.1
  18.3 2.6 collective-permute-start.1
  21.5 7.7 %fusion.32 = (f32[64,3,4,8,1]{4,3,2,1,0:T(8,128)}, f32[64,3,4,8,1]{4,3,2,1,0:T(8,128)}, f32[64,3,4,8,1]{4,3,2,1,0:T(8,128)}, f32[64,3,4,8,1]{4,3,2,1,0:T(8,128)}...) fusion(f32[64,3,4,8,256]{4,3,2,1,0:T(8,128)S(1)} %copy-done), kind=kLoop, calls=%fused_computation.59 | loop fusion | bytes 294912 | tf_op jit(solution)/shard_map/slice | solution.py:25
  29.2 2.7 copy.66
  31.9 2.7 copy.67
  34.6 2.7 copy.68
  37.2 2.7 copy.69
  39.9 2.7 copy.70
  44.0 2.3 copy.57
  46.3 2.5 copy.58
  48.8 2.5 copy.72
  51.3 9.2 %fusion = f32[64,3,4,8,254]{4,0,3,2,1:T(8,128)} fusion(f32[64,3,4,8,256]{4,0,3,2,1:T(8,128)} %copy-done.1), kind=kLoop, calls=%fused_computation.1 | loop fusion | flops 3121152 | bytes 18726912 | tf_op jit(solution)/shard_map/mul | solution.py:24
  60.5 7.3 %pad_maximum_fusion.4 = f32[64,3,4,8,256]{4,0,3,2,1:T(8,128)S(1)} fusion(f32[64,3,4,8,1]{4,0,3,2,1:T(8,128)} %copy.58, f32[64,3,4,8,254]{4,0,3,2,1:T(8,128)} %fusion, f32[64,3,4,8,1]{4,0,3,2,1:T(8,128)} %copy.57), kind=kLoop, calls=%fused_computation.10 | loop fusion | flops 3145728 | bytes 12582912 | tf_op jit(solution)/shard_map/concatenate | solution.py:27
  69.3 4.1 constant_dynamic-update-slice_fusion.1
  75.3 5.2 collective-permute-start.2
  82.0 12.6 %fusion.4 = f32[64,3,4,8,256]{4,0,3,2,1:T(8,128)S(1)} fusion(f32[64,3,4,8,256]{4,0,3,2,1:T(8,128)S(1)} %bitcast.38, f32[64,3,1,8,256]{4,0,3,2,1:T(8,128)} %collective-permute-done.1, f32[64,3,1,8,256]{4,0,3,2,1:T(8,128)} %collective-permute-done), kind=kLoop, calls=%fused_computation.8 | loop fusion | flops 6291456 | bytes 15728640 | tf_op jit(solution)/shard_map/mul | solution.py:40
  94.5 7.4 %collective-permute-done.2 = f32[64,3,6,1,256]{4,0,3,2,1:T(8,128)S(1)} collective-permute-done((f32[64,3,6,1,256]{4,0,3,2,1:T(8,128)S(1)}, f32[64,3,6,1,256]{4,0,3,2,1:T(8,128)S(1)}, u32[]{:S(2)}, u32[]{:S(2)}) %collective-permute-start.2) | collective-permute-done | bytes 1179680 | tf_op jit(solution)/shard_map/ppermute | solution.py:18
  102.0 3.1 collective-permute-done.3
  105.1 2.1 fusion.2
  109.3 2.6 copy.59
  115.0 7.6 %fusion.34 = f32[128,128]{0,1:T(8,128)} fusion(f32[128,8192]{1,0:T(8,128)} %constant_dynamic-update-slice_fusion.3), kind=kOutput, calls=%fused_computation.61 | convolution fusion | flops 1610612736 | bytes 4259840 | tf_op jit(solution)/shard_map/dot_general | solution.py:31
  122.7 243.7 %all-reduce.3.cloned.1.call-done = f32[128,128]{0,1:T(8,128)} async-done(((f32[128,128]{0,1:T(8,128)}), f32[128,128]{0,1:T(8,128)}) %all-reduce.3.cloned.1.call-update) | async-done | bytes 65552 | tf_op jit(solution)/shard_map/psum | solution.py:51
  368.2 11.7 %cholesky.44 = f32[128,128]{1,0:T(8,128)S(1)} custom-call(f32[128,128]{1,0:T(8,128)S(1)} %fusion.16), custom_call_target="Cholesky" | custom-call | tf_op jit(solution)/shard_map/jit(cholesky)/cholesky | solution.py:52
  381.3 9.8 %custom-call.6 = f32[1,128,128]{1,2,0:T(8,128)S(1)} custom-call(f32[1,128,128]{2,1,0:T(8,128)S(1)} %get-tuple-element.5), custom_call_target="InvertDiagBlocksLowerTriangular" | custom-call | tf_op jit(solution)/shard_map/triangular_solve/custom-call.0 | solution.py:53
  391.1 5.7 fusion.14
  398.8 4.0 fusion.35
  402.8 237.9 %all-reduce.5.cloned.1.call-done = f32[128,128]{0,1:T(8,128)} async-done(((f32[128,128]{0,1:T(8,128)}), f32[128,128]{0,1:T(8,128)}) %all-reduce.5.cloned.1.call-update) | async-done | bytes 65552 | tf_op jit(solution)/shard_map/psum | solution.py:54
  642.5 11.7 %cholesky.55 = f32[128,128]{1,0:T(8,128)S(1)} custom-call(f32[128,128]{1,0:T(8,128)S(1)} %fusion.13), custom_call_target="Cholesky" | custom-call | tf_op jit(solution)/shard_map/jit(cholesky)/cholesky | solution.py:55
  657.1 9.8 %custom-call.7 = f32[1,128,128]{1,2,0:T(8,128)S(1)} custom-call(f32[1,128,128]{2,1,0:T(8,128)S(1)} %select_bitcast_fusion), custom_call_target="InvertDiagBlocksLowerTriangular" | custom-call | tf_op jit(solution)/shard_map/triangular_solve/custom-call.0 | solution.py:56
  667.0 5.7 fusion.11
  672.7 3.3 copy.73
  (53 shorter events, 24.2 us)
Async XLA Ops:
  7.2 359.2 %all-reduce.3.cloned.1.call-start = ((), (), s32[]{:S(2)}) async-start(), calls=%async_computation | async-start | bytes 131072 | tf_op jit(solution)/shard_map/psum | solution.py:51
  13.6 2.7 copy-start.1
  16.3 5.2 copy-start
  18.3 49.5 %collective-permute-start.1 = (f32[64,3,1,8,256]{4,0,3,2,1:T(8,128)}, f32[64,3,1,8,256]{4,0,3,2,1:T(8,128)}, u32[]{:S(2)}, u32[]{:S(2)}) collective-permute-start(f32[64,3,1,8,256]{4,0,3,2,1:T(8,128)} %get-tuple-element.16), channel_id=1, source_target_pairs={{0,8},{8,16},{16,24},{24,32},{32,40},{40,48},{48,56},{56,64},{64,7... | collective-permute-start | bytes 4718600 | tf_op jit(solution)/shard_map/ppermute | solution.py:15
  20.9 52.5 %collective-permute-start = (f32[64,3,1,8,256]{4,0,3,2,1:T(8,128)}, f32[64,3,1,8,256]{4,0,3,2,1:T(8,128)}, u32[]{:S(2)}, u32[]{:S(2)}) collective-permute-start(f32[64,3,1,8,256]{4,0,3,2,1:T(8,128)} %get-tuple-element.15), channel_id=1, source_target_pairs={{8,0},{16,8},{24,16},{32,24},{40,32},{48,40},{56,48},{64,56},{72,6... | collective-permute-start | bytes 4718600 | tf_op jit(solution)/shard_map/ppermute | solution.py:18
  44.0 4.8 copy-start.4
  51.3 18.0 %slice-start = ((s8[6291456]{0:T(1024)(128)(4,1)}), s8[4194304]{0:T(1024)(128)(4,1)S(1)}, s32[]{:S(2)}) async-start(s8[6291456]{0:T(1024)(128)(4,1)} %bitcast.35), calls=%async_computation.2 | async-start | bytes 8388608
  60.5 8.8 %slice-start.1 = ((s8[6291456]{0:T(1024)(128)(4,1)}), s8[2097152]{0:T(1024)(128)(4,1)S(1)}, s32[]{:S(2)}) async-start(s8[6291456]{0:T(1024)(128)(4,1)} %bitcast.35), calls=%async_computation.3 | async-start | bytes 4194304
  73.4 7.1 %copy-start.3 = (f32[8,8,32,256]{3,1,2,0:T(8,128)S(1)}, f32[8,8,32,256]{3,1,2,0:T(8,128)}, u32[]{:S(2)}) copy-start(f32[8,8,32,256]{3,1,2,0:T(8,128)} %copy.72) | copy-start | bytes 6291460
  73.4 8.6 %slice-start.2 = ((s8[6291456]{0:T(1024)(128)(4,1)}), s8[4194304]{0:T(1024)(128)(4,1)S(1)}, s32[]{:S(2)}) async-start(s8[6291456]{0:T(1024)(128)(4,1)} %bitcast.37), calls=%async_computation.4 | async-start | bytes 8388608
  75.1 6.9 %slice-start.3 = ((s8[6291456]{0:T(1024)(128)(4,1)}), s8[2097152]{0:T(1024)(128)(4,1)S(1)}, s32[]{:S(2)}) async-start(s8[6291456]{0:T(1024)(128)(4,1)} %bitcast.37), calls=%async_computation.5 | async-start | bytes 4194304
  75.3 26.6 %collective-permute-start.2 = (f32[64,3,6,1,256]{4,0,3,2,1:T(8,128)S(1)}, f32[64,3,6,1,256]{4,0,3,2,1:T(8,128)S(1)}, u32[]{:S(2)}, u32[]{:S(2)}) collective-permute-start(f32[64,3,6,1,256]{4,0,3,2,1:T(8,128)S(1)} %get-tuple-element.7), channel_id=1, source_target_pairs={{1,0},{2,1},{3,2},{4,3},{5,4},{6,5},{7,6},{0,7},{9,8},{10,9},{11,1... | collective-permute-start | bytes 3538952 | tf_op jit(solution)/shard_map/ppermute | solution.py:18
  80.5 24.6 %collective-permute-start.3 = (f32[64,3,6,1,256]{4,0,3,2,1:T(8,128)S(1)}, f32[64,3,6,1,256]{4,0,3,2,1:T(8,128)S(1)}, u32[]{:S(2)}, u32[]{:S(2)}) collective-permute-start(f32[64,3,6,1,256]{4,0,3,2,1:T(8,128)S(1)} %get-tuple-element.8), channel_id=1, source_target_pairs={{0,1},{1,2},{2,3},{3,4},{4,5},{5,6},{6,7},{7,0},{8,9},{9,10},{10,1... | collective-permute-start | bytes 3538952 | tf_op jit(solution)/shard_map/ppermute | solution.py:15
  122.7 518.0 %all-reduce.5.cloned.1.call-start = ((), (), s32[]{:S(2)}) async-start(), calls=%async_computation.1 | async-start | bytes 131072 | tf_op jit(solution)/shard_map/psum | solution.py:54
  381.3 274.3 %copy-start.5 = (f32[128,128]{1,0:T(8,128)}, f32[128,128]{1,0:T(8,128)S(1)}, u32[]{:S(2)}) copy-start(f32[128,128]{1,0:T(8,128)S(1)} %get-tuple-element.6) | copy-start | bytes 196612
  396.7 2.0 copy-start.2
Sparse Core Ops, SparseCore 0:
  122.8 243.5 all-reduce.2
  402.9 237.7 all-reduce.4
where the time goes:
time: 692 us; the launch traced here: 683 us
  waiting for transfers between devices  492 us (71%)
  other arithmetic  82.3 us (12%)
  local copies, waits for them, and re-layouts  61 us (9%)
  matrix products  24.5 us (4%)
  between operations  14.8 us (2%)
  starting transfers between devices  8.45 us (1%)
    psum x1, waiting for transfers between devices, shards(): gram_sum = lax.psum(product(stacked, stacked), ('gx', 'gz'))  244 us
    psum x1, waiting for transfers between devices, shards(): second_sum = lax.psum(product(first_pass, first_pass), ('gx', 'gz'))  238 us
    unnamed x32, local copies, waits for them, and re-layouts  38.8 us
  transfers between devices with their start and end apart: 6, of which 4 were waited for; matrix products, arithmetic and copies ran while one was open for 10% of the time, Pallas kernels for 0%

commit v1 on v0

v1 whole, which is shorter than its diff:
```python
import jax
import jax.numpy as jnp
from jax import lax
from jax.experimental import pallas as pl
from jax.experimental.pallas import tpu as pltpu
from jax.sharding import PartitionSpec as P

precise = lax.Precision.HIGHEST
LANES = 128


def pack_faces(velocity, group=16):
    snaps, comps, nx, nz, ny = velocity.shape
    halves = ny // LANES
    rows = group * comps * nx

    def kernel(*refs):
        views, (first_x, last_x, first_z, last_z) = refs[:halves], refs[halves:]
        for h, v_ref in enumerate(views):
            lanes = slice(h * LANES, (h + 1) * LANES)
            first_x[:, :, :, lanes] = v_ref[:, :, 0]
            last_x[:, :, :, lanes] = v_ref[:, :, nx - 1]
            flat = v_ref.reshape(rows * nz, LANES)
            first_z[h] = flat[pl.ds(0, rows, stride=nz), :]
            last_z[h] = flat[pl.ds(nz - 1, rows, stride=nz), :]

    face_x = jax.ShapeDtypeStruct((snaps, comps, nz, ny), velocity.dtype)
    face_z = jax.ShapeDtypeStruct((halves, snaps * comps * nx, LANES), velocity.dtype)
    spec_x = pl.BlockSpec((group, comps, nz, ny), lambda i: (i, 0, 0, 0))
    spec_z = pl.BlockSpec((halves, rows, LANES), lambda i: (0, i, 0))
    block = (group, comps, nx, nz, LANES)
    return pl.pallas_call(
        kernel,
        grid=(snaps // group,),
        in_specs=[pl.BlockSpec(block, lambda i, h=h: (i, 0, 0, 0, h)) for h in range(halves)],
        out_specs=[spec_x, spec_x, spec_z, spec_z],
        out_shape=[face_x, face_x, face_z, face_z],
        name="pack_faces",
    )(*[velocity] * halves)


def flatten_modes(modes, group=2):
    count, nx, nz, ny = modes.shape
    halves = ny // LANES

    def kernel(*refs):
        out_ref = refs[halves]
        for h in range(halves):
            flat = refs[h].reshape(count * group * nz, LANES)
            for x in range(group):
                for z in range(nz):
                    start = ((x * halves + h) * nz + z) * LANES
                    out_ref[:, start : start + LANES] = flat[pl.ds(x * nz + z, count, stride=group * nz), :]

    block = (count, group, nz, LANES)
    return pl.pallas_call(
        kernel,
        grid=(nx // group,),
        in_specs=[pl.BlockSpec(block, lambda i, h=h: (0, i, 0, h)) for h in range(halves)],
        out_specs=pl.BlockSpec((count, group * nz * ny), lambda i: (0, i)),
        out_shape=jax.ShapeDtypeStruct((count, nx * nz * ny), modes.dtype),
        name="flatten_modes",
    )(*[modes] * halves)


def criterion(velocity, low_x, high_x, low_z, high_z, group=8):
    snaps, comps, nx, nz, ny = velocity.shape
    rows = group * comps * nx
    halves = ny // LANES

    def kernel(v_ref, lx_ref, hx_ref, lz_ref, hz_ref, out_ref, q_ref):
        lane = lax.broadcasted_iota(jnp.int32, (nz, LANES), 1)
        level = lax.broadcasted_iota(jnp.int32, (nz, LANES), 0)

        def cut(half):
            return slice(half * LANES, (half + 1) * LANES)

        def wall(parts):
            below = [pltpu.roll(p, 1, 1) for p in parts]
            above = [pltpu.roll(p, LANES - 1, 1) for p in parts]
            out = []
            for h in range(halves):
                fm = jnp.where(lane == 0, below[h - 1], below[h]) if h else below[h]
                fp = jnp.where(lane == LANES - 1, above[h + 1], above[h]) if h < halves - 1 else above[h]
                d = fp - fm
                if h == 0:
                    d = jnp.where(lane == 0, -3.0 * parts[h] + 4.0 * fp - pltpu.roll(parts[h], LANES - 2, 1), d)
                if h == halves - 1:
                    d = jnp.where(lane == LANES - 1, 3.0 * parts[h] - 4.0 * fm + pltpu.roll(parts[h], 2, 1), d)
                out.append(d)
            return out

        def body(s, carry):
            for x in range(nx):
                dx, dz, dy = [], [], []
                for c in range(comps):
                    here = [v_ref[s, c, x, :, cut(h)] for h in range(halves)]
                    dx.append([
                        (v_ref[s, c, x + 1, :, cut(h)] if x < nx - 1 else hx_ref[s, c, :, cut(h)])
                        - (v_ref[s, c, x - 1, :, cut(h)] if x else lx_ref[s, c, :, cut(h)])
                        for h in range(halves)
                    ])
                    row = (s * comps + c) * nx + x
                    part = []
                    for h in range(halves):
                        up = jnp.where(level == nz - 1, hz_ref.at[h][pl.ds(row, nz, stride=0), :], pltpu.roll(here[h], nz - 1, 0))
                        down = jnp.where(level == 0, lz_ref.at[h][pl.ds(row, nz, stride=0), :], pltpu.roll(here[h], 1, 0))
                        part.append(up - down)
                    dz.append(part)
                    dy.append(wall(here))
                for h in range(halves):
                    diagonal = dx[0][h] * dx[0][h] + dz[1][h] * dz[1][h] + dy[2][h] * dy[2][h]
                    cross = dz[0][h] * dx[1][h] + dy[0][h] * dx[2][h] + dy[1][h] * dz[2][h]
                    q_ref[h, pl.ds((s * nx + x) * nz, nz), :] = -0.125 * diagonal - 0.25 * cross
            return carry

        lax.fori_loop(0, group, body, 0)
        for x in range(nx):
            for z in range(nz):
                for h in range(halves):
                    start = ((x * halves + h) * nz + z) * LANES
                    view = q_ref.at[h]
                    out_ref[:, start : start + LANES] = view[pl.ds(x * nz + z, group, stride=nx * nz), :]

    spec_x = pl.BlockSpec((group, comps, nz, ny), lambda i: (i, 0, 0, 0))
    spec_z = pl.BlockSpec((halves, rows, LANES), lambda i: (0, i, 0))
    return pl.pallas_call(
        kernel,
        grid=(snaps // group,),
        in_specs=[pl.BlockSpec((group, comps, nx, nz, ny), lambda i: (i, 0, 0, 0, 0)), spec_x, spec_x, spec_z, spec_z],
        out_specs=pl.BlockSpec((group, nx * nz * ny), lambda i: (i, 0)),
        out_shape=jax.ShapeDtypeStruct((snaps, nx * nz * ny), velocity.dtype),
        scratch_shapes=[pltpu.VMEM((halves, group * nx * nz, LANES), velocity.dtype)],
        name="criterion",
    )(velocity, low_x, high_x, low_z, high_z)


def spread(row, shape):
    return jnp.broadcast_to(row, shape)


def three_parts(value):
    first = value.astype(jnp.bfloat16).astype(jnp.float32)
    rest = value - first
    second = rest.astype(jnp.bfloat16).astype(jnp.float32)
    return first, second, rest - second


def eliminate(a_ref, x_ref, u_ref):
    size = a_ref.shape[0]
    tall = 8
    row = lax.broadcasted_iota(jnp.int32, (tall, size), 0)
    lane = lax.broadcasted_iota(jnp.int32, (tall, size), 1)
    full = (tall, size)
    full_row = lax.broadcasted_iota(jnp.int32, (size, size), 0)
    full_lane = lax.broadcasted_iota(jnp.int32, (size, size), 1)
    x_ref[...] = jnp.where(full_row == full_lane, 1.0, 0.0)
    for start in range(0, size, tall):
        rows = slice(start, start + tall)
        left, right = a_ref[rows, :], x_ref[rows, :]
        columns = [spread(left[:, start + j : start + j + 1], full) for j in range(tall)]
        pivots = jnp.ones(full, jnp.float32)
        for j in range(tall):
            pivot = spread(columns[j][j : j + 1, :], full)
            pivots = jnp.where(row == j, pivot, pivots)
            if j == tall - 1:
                break
            factor = jnp.where(row > j, columns[j] * (1.0 / pivot), 0.0)
            for k in range(j + 1, tall):
                columns[k] = columns[k] - factor * spread(columns[k][j : j + 1, :], full)
            left = left - factor * spread(left[j : j + 1, :], full)
            right = right - factor * spread(right[j : j + 1, :], full)
        scale = 1.0 / jnp.sqrt(pivots)
        left = jnp.where(lane >= start + row, left * scale, 0.0)
        right = right * scale
        u_ref[rows, :] = left
        x_ref[rows, :] = right
        if start + tall < size:
            l1, l2, l3 = three_parts(left)
            r1, r2, r3 = three_parts(right)
            lhs = jnp.concatenate([l1, l1, l2, l2, l1, l3], 0).astype(jnp.bfloat16)
            rhs_left = jnp.concatenate([l1, l2, l1, l2, l3, l1], 0).astype(jnp.bfloat16)
            rhs_right = jnp.concatenate([r1, r2, r1, r2, r3, r1], 0).astype(jnp.bfloat16)
            rhs = jnp.concatenate([rhs_left, rhs_right], 1)
            change = lax.dot_general(lhs, rhs, (((0,), (0,)), ((), ())), preferred_element_type=jnp.float32)
            below = slice(start + tall, size)
            a_ref[below, :] -= change[start + tall :, :size]
            x_ref[below, :] -= change[start + tall :, size:]


def matmul(left, right, dims=((1,), (0,))):
    return lax.dot_general(left, right, (dims, ((), ())), precision=precise, preferred_element_type=jnp.float32)


def split(value, top):
    big = top * (1.5 * 2.0**16)
    first = (value + big) - big
    rest = value - first
    second = rest.astype(jnp.bfloat16).astype(jnp.float32)
    rest = rest - second
    third = rest.astype(jnp.bfloat16).astype(jnp.float32)
    return first, second, third, rest - third


def residual(gram, upper):
    parts = [p.astype(jnp.bfloat16) for p in split(upper, jnp.max(jnp.abs(upper), 0, keepdims=True))]

    def cross(i, j):
        return lax.dot_general(parts[i], parts[j], (((0,), (0,)), ((), ())), preferred_element_type=jnp.float32)

    out = gram - cross(0, 0)
    both = cross(1, 0)
    out = out - (both + both.T)
    both = cross(2, 0) + (cross(3, 0) + cross(2, 1))
    return out - (cross(1, 1) + (both + both.T))


def factor(mine, other, core, cells):
    size = mine.shape[2]
    half = size // 2
    quarter = half // 2

    def kernel(core_ref, mine_ref, other_ref, weight_ref, triangle_ref, lower_ref, a_ref, x_ref, u_ref, y_ref, v_ref):
        full_row = lax.broadcasted_iota(jnp.int32, (size, size), 0)
        full_lane = lax.broadcasted_iota(jnp.int32, (size, size), 1)
        first = core_ref[0] == 0

        def whole(k):
            low = jnp.where(first, mine_ref[k], other_ref[k])
            high = jnp.where(first, other_ref[k], mine_ref[k])
            corner = jnp.concatenate([low[quarter:], high[quarter:]], 0)
            rows = jnp.concatenate([low[:quarter], high[:quarter], pltpu.roll(corner, half, 1), corner], 0)
            rows = rows * (1.0 / cells)
            return jnp.where(full_lane >= full_row, rows, rows.T)

        gram, extra = whole(0), whole(1)
        a_ref[...] = gram
        eliminate(a_ref, x_ref, u_ref)
        upper = u_ref[...]
        eye = jnp.where(full_row == full_lane, 1.0, 0.0)
        inverse = refined(x_ref[...], upper, eye)
        lower_ref[...] = upper.T
        rest = residual(gram, upper) + extra
        change = matmul(matmul(inverse, rest), inverse, ((1,), (1,)))
        change = jnp.where(full_lane <= full_row, change, change.T)
        small = jnp.sum(change * change) < 2.0**-18

        @pl.when(small)
        def _():
            keep = jnp.where(full_lane < full_row, 1.0, jnp.where(full_lane == full_row, 0.5, 0.0))
            step = keep * change
            step = keep * (change - matmul(step, step, ((1,), (1,))))
            weight_ref[...] = inverse - matmul(step, inverse - matmul(step, inverse))
            triangle_ref[...] = upper + matmul(step, upper, ((0,), (0,)))

        @pl.when(jnp.logical_not(small))
        def _():
            a_ref[...] = change + eye
            eliminate(a_ref, y_ref, v_ref)
            weight_ref[...] = matmul(refined(y_ref[...], v_ref[...], eye), inverse)
            triangle_ref[...] = matmul(v_ref[...], upper)

    square = jax.ShapeDtypeStruct((size, size), jnp.float32)
    vmem = pl.BlockSpec(memory_space=pltpu.VMEM)
    return pl.pallas_call(
        kernel,
        in_specs=[pl.BlockSpec(memory_space=pltpu.SMEM), vmem, vmem],
        out_specs=[vmem, vmem, vmem],
        out_shape=[square, square, square],
        scratch_shapes=[pltpu.VMEM((size, size), jnp.float32)] * 5,
        name="factor",
    )(core, mine, other)


def refined(inverse, upper, eye):
    return inverse + matmul(eye - matmul(inverse, upper, ((1,), (1,))), inverse)


def two_sum(left, right):
    total = left + right
    back = total - left
    return total, (left - (total - back)) + (right - back)


def gram_halves(modes, fields, core, chunk=2048, piece=512):
    old, cells = modes.shape
    new = fields.shape[0]
    size = old + new
    half, quarter = size // 2, size // 4
    steps = cells // chunk

    def kernel(core_ref, m_ref, f_ref, keep_ref, send_ref, high_ref, low_ref, cross_ref):
        step = pl.program_id(0)

        @pl.when(step == 0)
        def _():
            high_ref[...] = jnp.zeros_like(high_ref)
            low_ref[...] = jnp.zeros_like(low_ref)
            cross_ref[...] = jnp.zeros_like(cross_ref)

        for k in range(chunk // piece):
            span = slice(k * piece, (k + 1) * piece)
            block = jnp.concatenate([m_ref[:, span], f_ref[:, span]], 0)
            first, second, third, _ = split(block, jnp.max(jnp.abs(block), 1, keepdims=True))
            lhs = jnp.concatenate([first, second, third], 0).astype(jnp.bfloat16)
            part = lax.dot_general(
                lhs, lhs[: 2 * size], (((1,), (1,)), ((), ())), preferred_element_type=jnp.float32
            )
            high_ref[...], error = two_sum(high_ref[...], part[:size, :size])
            low_ref[...] += error + part[size : 2 * size, size:]
            cross_ref[...] += part[size : 2 * size, :size] + (part[2 * size :, :size] + part[2 * size :, size:])

        @pl.when(step == steps - 1)
        def _():
            cross = cross_ref[...]
            high_ref[...], low_ref[...] = two_sum(high_ref[...], low_ref[...] + (cross + cross.T))
            lane = lax.broadcasted_iota(jnp.int32, (quarter, size), 1)
            lead = core_ref[0] == 0
            for k, ref in enumerate((high_ref, low_ref)):
                corner = jnp.where(lane < half, pltpu.roll(ref[half : half + quarter, :], half, 1), ref[half + quarter :, :])
                low = jnp.concatenate([ref[:quarter, :], corner[: quarter // 2]], 0)
                high = jnp.concatenate([ref[quarter:half, :], corner[quarter // 2 :]], 0)
                keep_ref[k] = jnp.where(lead, low, high)
                send_ref[k] = jnp.where(lead, high, low)

    out = jax.ShapeDtypeStruct((2, quarter + quarter // 2, size), jnp.float32)
    spec = pl.BlockSpec((2, quarter + quarter // 2, size), lambda i: (0, 0, 0))
    return pl.pallas_call(
        kernel,
        grid=(steps,),
        in_specs=[
            pl.BlockSpec(memory_space=pltpu.SMEM),
            pl.BlockSpec((old, chunk), lambda i: (0, i)),
            pl.BlockSpec((new, chunk), lambda i: (0, i)),
        ],
        out_specs=[spec, spec],
        out_shape=[out, out],
        scratch_shapes=[pltpu.VMEM((size, size), jnp.float32)] * 3,
        name="gram_halves",
    )(core, modes, fields)


def apply_split(weight, modes, fields, nx, nz, ny):
    old, cells = modes.shape
    new = fields.shape[0]
    count = old + new
    halves = ny // LANES

    def kernel(w_ref, m_ref, f_ref, out_ref):
        w1, w2, w3 = three_parts(w_ref[...])
        lhs = jnp.concatenate(
            [
                jnp.concatenate([w1, w2], 1),
                jnp.concatenate([w2, w1], 1),
                jnp.concatenate([w3, jnp.zeros_like(w3)], 1),
            ],
            0,
        ).astype(jnp.bfloat16)
        block = jnp.concatenate([m_ref[...], f_ref[...]], 0)
        s1, s2, s3 = three_parts(block)
        pair = jnp.concatenate([s1, s2], 0).astype(jnp.bfloat16)
        dims = (((1,), (0,)), ((), ()))
        main = lax.dot_general(lhs, pair, dims, preferred_element_type=jnp.float32)
        tail = lax.dot_general(w1.astype(jnp.bfloat16), s3.astype(jnp.bfloat16), dims, preferred_element_type=jnp.float32)
        result = main[:count] + (main[count : 2 * count] + (main[2 * count :] + tail))
        flat = out_ref.reshape(count * nz, LANES)
        for z in range(nz):
            flat[pl.ds(z, count, stride=nz), :] = result[:, z * LANES : (z + 1) * LANES]

    return pl.pallas_call(
        kernel,
        grid=(nx, halves),
        in_specs=[
            pl.BlockSpec((count, count), lambda i, h: (0, 0)),
            pl.BlockSpec((old, nz * LANES), lambda i, h: (0, i * halves + h)),
            pl.BlockSpec((new, nz * LANES), lambda i, h: (0, i * halves + h)),
        ],
        out_specs=pl.BlockSpec((count, 1, nz, LANES), lambda i, h: (0, i, 0, h)),
        out_shape=jax.ShapeDtypeStruct((count, nx, nz, ny), jnp.float32),
        name="apply_split",
    )(weight, modes, fields)


def shifted(value, axis, forward):
    count = lax.axis_size(axis)
    step = 1 if forward else count - 1
    return lax.ppermute(value, axis, [(i, (i + step) % count) for i in range(count)])


def flipped(value, flip_x, flip_z):
    size_x, size_z = lax.axis_size("gx"), lax.axis_size("gz")
    pairs = [
        (x * size_z + z, (x ^ flip_x) * size_z + (z ^ flip_z)) for x in range(size_x) for z in range(size_z)
    ]
    return lax.ppermute(value, ("gx", "gz"), pairs)


def pair_sum(left, right):
    high, error = two_sum(left[0], right[0])
    return jnp.stack([high, left[1] + right[1] + error])


def all_sum(keep, send):
    value = pair_sum(keep, flipped(send, 1, 0))
    flips = [(1 << bit, 0) for bit in range(1, lax.axis_size("gx").bit_length() - 1)]
    flips += [(0, 1 << bit) for bit in range(lax.axis_size("gz").bit_length() - 1)]
    for flip_x, flip_z in flips:
        value = pair_sum(value, flipped(value, flip_x, flip_z))
    return value, flipped(value, 1, 0)


def shards(velocity, scaled_modes):
    _, _, cells_x, cells_z, cells_y = velocity.shape
    total_cells = cells_x * lax.axis_size("gx") * cells_z * lax.axis_size("gz") * cells_y
    core = (lax.axis_index("gx") % 2).astype(jnp.int32).reshape(1)
    first_x, last_x, first_z, last_z = pack_faces(velocity)
    low_x, high_x = shifted(last_x, "gx", True), shifted(first_x, "gx", False)
    low_z, high_z = shifted(last_z, "gz", True), shifted(first_z, "gz", False)
    modes = flatten_modes(scaled_modes)
    fields = criterion(velocity, low_x, high_x, low_z, high_z)
    mine, other = all_sum(*gram_halves(modes, fields, core))
    weight, triangle, lower_one = factor(mine, other, core, float(total_cells))
    basis = apply_split(weight, modes, fields, cells_x, cells_z, cells_y)
    return basis, triangle, lower_one


def solution(mesh):
    in_specs = (P(None, None, "gx", "gz", None), P(None, "gx", "gz", None))
    out_specs = (P(None, "gx", "gz", None), P(), P())
    return jax.shard_map(shards, mesh=mesh, in_specs=in_specs, out_specs=out_specs, check_vma=False)
```

time: 692 us -> 121 us (0.17); the launches traced: 683 us -> 120 us
  waiting for transfers between devices: 492 us -> 27.7 us
  other arithmetic: 82.3 us -> 0.91 us
  local copies, waits for them, and re-layouts: 61 us -> 2.35 us
  Pallas kernels: 0 us -> 50.9 us
  starting transfers between devices: 8.45 us -> 37.4 us
  matrix products: 24.5 us -> 0 us
  between operations: 14.8 us -> 0.75 us
    psum x2 -> x0, waiting for transfers between devices: 482 us -> none  [the longest x1 244 us: shards(): gram_sum = lax.psum(product(stacked, stacked), ('gx', 'gz'))]
    pallas_call x0 -> x6, Pallas kernels: none -> 50.9 us  [the longest x1 15.5 us: factor(): pl.pallas_call(kernel, in_specs=[pl.BlockSpec(memory_space=pltpu.SMEM), v...]
    another operation x10 -> x8, other arithmetic: 45.7 us -> 0.05 us  [pair_sum(): return jnp.stack([high, left[1] + right[1] + error])]
    unnamed x32 -> x8, local copies, waits for them, and re-layouts: 38.8 us -> 2.35 us
    ppermute x4 -> x13, starting transfers between devices: 8.37 us -> 37.4 us  [the longest x9 29.2 us: flipped(): return lax.ppermute(value, ('gx', 'gz'), pairs)]
    mul x5 -> x0, other arithmetic: 23.9 us -> none  [the longest x1 12.6 us: shards(): grad_x = (padded[:, :, 2:, 1:-1] - padded[:, :, :-2, 1:-1]) * 0.5]
    ppermute x4 -> x13, waiting for transfers between devices: 10.6 us -> 27.7 us  [the longest x9 15.8 us: flipped(): return lax.ppermute(value, ('gx', 'gz'), pairs)]
    dot_general x3 -> x0, matrix products: 13.2 us -> none  [the longest x2 11.6 us: product(): lax.dot_general(left, right, (((1,), (1,)), ((), ())), precision=precise)]
  transfers between devices with their start and end apart: 6 -> 13, of which waited for: 4 -> 11; matrix products, arithmetic and copies ran while one was open for 10% -> 0% of each run, Pallas kernels for 0% -> 2%
where the time goes in v1:
time: 121 us; the launch traced here: 120 us
  Pallas kernels  50.9 us (42%)
  starting transfers between devices  37.4 us (31%)
  waiting for transfers between devices  27.7 us (23%)
  local copies, waits for them, and re-layouts  2.35 us (2%)
    ppermute x9, starting transfers between devices, flipped(): return lax.ppermute(value, ('gx', 'gz'), pairs)  29.2 us
    ppermute x9, waiting for transfers between devices, flipped(): return lax.ppermute(value, ('gx', 'gz'), pairs)  15.8 us
    pallas_call x1, Pallas kernels, factor(): pl.pallas_call(kernel, in_specs=[pl.BlockSpec(memory_space=pltpu.SMEM), v...  15.5 us
    pallas_call x1, Pallas kernels, criterion(): pl.pallas_call(kernel, grid=(snaps // group,), in_specs=[pl.BlockSpec((gr...  13.4 us
    ppermute x4, waiting for transfers between devices, shifted(): lax.ppermute(value, axis, [(i, (i + step) % count) for i in range(count)])  12 us
    ppermute x4, starting transfers between devices, shifted(): lax.ppermute(value, axis, [(i, (i + step) % count) for i in range(count)])  8.17 us
    pallas_call x1, Pallas kernels, apply_split(): pl.pallas_call(kernel, grid=(nx, halves), in_specs=[pl.BlockSpec((count,...  8.11 us
    pallas_call x1, Pallas kernels, gram_halves(): pl.pallas_call(kernel, grid=(steps,), in_specs=[pl.BlockSpec(memory_space...  5.6 us
  transfers between devices with their start and end apart: 13, of which 11 were waited for; matrix products, arithmetic and copies ran while one was open for 0% of the time, Pallas kernels for 2%

profile of v1, /device:TPU:1, one launch (start us, length us, event | category | flops | bytes accessed | tf_op | source)
XLA Modules:
  0.0 120.1 jit_solution(572839305990766309)
XLA Ops:
  0.6 5.4 %pack_faces.1 = (f32[64,3,8,256]{3,2,1,0:T(8,128)}, f32[64,3,8,256]{3,2,1,0:T(8,128)}, f32[2,768,128]{2,1,0:T(8,128)}, f32[2,768,128]{2,1,0:T(8,128)}) custom-call(f32[64,3,4,8,256]{4,3,2,1,0:T(8,128)} %v_ref.1, f32[64,3,4,8,256]{4,3,2,1,0:T(8,128)} %v_ref.1), custom_call_target="tpu_custom_call" | custom-call | tf_op jit(solution)/shard_map/pack_faces/pallas_call | solution.py:32
  6.1 2.6 %collective-permute-start = (f32[64,3,8,256]{3,2,1,0:T(8,128)}, f32[64,3,8,256]{3,2,1,0:T(8,128)S(1)}, u32[]{:S(2)}, u32[]{:S(2)}) collective-permute-start(f32[64,3,8,256]{3,2,1,0:T(8,128)} %get-tuple-element.12), channel_id=1, source_target_pairs={{0,8},{8,16},{16,24},{24,32},{32,40},{40,48},{48,56},{56,64},{64,7... | collective-permute-start | bytes 4718600 | tf_op jit(solution)/shard_map/ppermute | solution.py:387
  8.6 0.7 collective-permute-start.1
  9.3 1.0 collective-permute-start.2
  10.3 3.9 %collective-permute-start.3 = (f32[2,768,128]{2,1,0:T(8,128)}, f32[2,768,128]{2,1,0:T(8,128)}, u32[]{:S(2)}, u32[]{:S(2)}) collective-permute-start(f32[2,768,128]{2,1,0:T(8,128)} %get-tuple-element.15), channel_id=1, source_target_pairs={{0,7},{1,0},{2,1},{3,2},{4,3},{5,4},{6,5},{7,6},{8,15},{9,8},{10,9... | collective-permute-start | bytes 2359304 | tf_op jit(solution)/shard_map/ppermute | solution.py:387
  14.2 2.9 %flatten_modes.1.m_ref = f32[64,8192]{1,0:T(8,128)} custom-call(f32[64,4,8,256]{3,2,1,0:T(8,128)} %refs_1_.2, f32[64,4,8,256]{3,2,1,0:T(8,128)} %refs_1_.2), custom_call_target="tpu_custom_call" | custom-call | tf_op jit(solution)/shard_map/flatten_modes/pallas_call | solution.py:56
  17.1 11.4 %collective-permute-done.2.lz_ref = f32[2,768,128]{2,1,0:T(8,128)} collective-permute-done((f32[2,768,128]{2,1,0:T(8,128)}, f32[2,768,128]{2,1,0:T(8,128)}, u32[]{:S(2)}, u32[]{:S(2)}) %collective-permute-start.2) | collective-permute-done | bytes 786464 | tf_op jit(solution)/shard_map/ppermute | solution.py:387
  28.5 0.6 collective-permute-done.1.hx_ref
  29.7 1.1 copy-done.1
  30.8 13.4 %criterion.1.f_ref = f32[64,8192]{1,0:T(8,128)} custom-call(f32[64,3,4,8,256]{4,3,2,1,0:T(8,128)} %v_ref.1, f32[64,3,8,256]{3,2,1,0:T(8,128)} %copy-done, f32[64,3,8,256]{3,2,1,0:T(8,128)} %copy-done.1, f32[2,768,128]{2,1,0:T(8,128)} %collective-permute-done.2.lz_ref, f32[2,768,128]{2,1,0:T(8,128)} %collective-permute-done.3.hz_ref), custom_call_target="tpu_custom_call" | custom-call | tf_op jit(solution)/shard_map/criterion/pallas_call | solution.py:127
  44.2 5.6 %gram_halves.1 = (f32[2,48,128]{2,1,0:T(8,128)}, f32[2,48,128]{2,1,0:T(8,128)}) custom-call(s32[1]{0:T(128)} %bitcast.core_ref, f32[64,8192]{1,0:T(8,128)} %flatten_modes.1.m_ref, f32[64,8192]{1,0:T(8,128)} %criterion.1.f_ref), custom_call_target="tpu_custom_call" | custom-call | tf_op jit(solution)/shard_map/gram_halves/pallas_call | solution.py:328
  49.8 4.5 %collective-permute-start.4 = (f32[2,48,128]{2,1,0:T(8,128)}, f32[2,48,128]{2,1,0:T(8,128)S(1)}, u32[]{:S(2)}, u32[]{:S(2)}) collective-permute-start(f32[2,48,128]{2,1,0:T(8,128)} %get-tuple-element.17), channel_id=1, source_target_pairs={{0,8},{1,9},{2,10},{3,11},{4,12},{5,13},{6,14},{7,15},{8,0},{9,1},... | collective-permute-start | bytes 147464 | tf_op jit(solution)/shard_map/ppermute | solution.py:395
  54.3 1.1 collective-permute-done.4
  55.4 0.8 fusion.7
  56.2 1.3 %collective-permute-start.5 = (f32[2,48,128]{2,1,0:T(8,128)S(1)}, f32[2,48,128]{2,1,0:T(8,128)S(1)}, u32[]{:S(2)}, u32[]{:S(2)}) collective-permute-start(f32[2,48,128]{2,1,0:T(8,128)S(1)} %pad_maximum_fusion), channel_id=1, source_target_pairs={{0,16},{1,17},{2,18},{3,19},{4,20},{5,21},{6,22},{7,23},{8,24},{9,... | collective-permute-start | bytes 147464 | tf_op jit(solution)/shard_map/ppermute | solution.py:395
  57.5 1.7 %collective-permute-done.5 = f32[2,48,128]{2,1,0:T(8,128)S(1)} collective-permute-done((f32[2,48,128]{2,1,0:T(8,128)S(1)}, f32[2,48,128]{2,1,0:T(8,128)S(1)}, u32[]{:S(2)}, u32[]{:S(2)}) %collective-permute-start.5) | collective-permute-done | bytes 49184 | tf_op jit(solution)/shard_map/ppermute | solution.py:395
  59.3 2.5 %collective-permute-start.6 = (f32[2,48,128]{2,1,0:T(8,128)S(1)}, f32[2,48,128]{2,1,0:T(8,128)S(1)}, u32[]{:S(2)}, u32[]{:S(2)}) collective-permute-start(f32[2,48,128]{2,1,0:T(8,128)S(1)} %pad_maximum_fusion.1), channel_id=1, source_target_pairs={{0,32},{1,33},{2,34},{3,35},{4,36},{5,37},{6,38},{7,39},{8,40},{9,... | collective-permute-start | bytes 147464 | tf_op jit(solution)/shard_map/ppermute | solution.py:395
  61.8 2.0 %collective-permute-done.6 = f32[2,48,128]{2,1,0:T(8,128)S(1)} collective-permute-done((f32[2,48,128]{2,1,0:T(8,128)S(1)}, f32[2,48,128]{2,1,0:T(8,128)S(1)}, u32[]{:S(2)}, u32[]{:S(2)}) %collective-permute-start.6) | collective-permute-done | bytes 49184 | tf_op jit(solution)/shard_map/ppermute | solution.py:395
  63.8 1.4 %collective-permute-start.7 = (f32[2,48,128]{2,1,0:T(8,128)S(1)}, f32[2,48,128]{2,1,0:T(8,128)S(1)}, u32[]{:S(2)}, u32[]{:S(2)}) collective-permute-start(f32[2,48,128]{2,1,0:T(8,128)S(1)} %pad_maximum_fusion.2), channel_id=1, source_target_pairs={{0,64},{1,65},{2,66},{3,67},{4,68},{5,69},{6,70},{7,71},{8,72},{9,... | collective-permute-start | bytes 147464 | tf_op jit(solution)/shard_map/ppermute | solution.py:395
  65.2 1.6 %collective-permute-done.7 = f32[2,48,128]{2,1,0:T(8,128)S(1)} collective-permute-done((f32[2,48,128]{2,1,0:T(8,128)S(1)}, f32[2,48,128]{2,1,0:T(8,128)S(1)}, u32[]{:S(2)}, u32[]{:S(2)}) %collective-permute-start.7) | collective-permute-done | bytes 49184 | tf_op jit(solution)/shard_map/ppermute | solution.py:395
  66.9 3.0 %collective-permute-start.8 = (f32[2,48,128]{2,1,0:T(8,128)S(1)}, f32[2,48,128]{2,1,0:T(8,128)S(1)}, u32[]{:S(2)}, u32[]{:S(2)}) collective-permute-start(f32[2,48,128]{2,1,0:T(8,128)S(1)} %pad_maximum_fusion.3), channel_id=1, source_target_pairs={{0,128},{1,129},{2,130},{3,131},{4,132},{5,133},{6,134},{7,135},{8... | collective-permute-start | bytes 147464 | tf_op jit(solution)/shard_map/ppermute | solution.py:395
  69.9 1.5 %collective-permute-done.8 = f32[2,48,128]{2,1,0:T(8,128)S(1)} collective-permute-done((f32[2,48,128]{2,1,0:T(8,128)S(1)}, f32[2,48,128]{2,1,0:T(8,128)S(1)}, u32[]{:S(2)}, u32[]{:S(2)}) %collective-permute-start.8) | collective-permute-done | bytes 49184 | tf_op jit(solution)/shard_map/ppermute | solution.py:395
  71.6 2.9 %collective-permute-done.9 = f32[2,48,128]{2,1,0:T(8,128)S(1)} collective-permute-done((f32[2,48,128]{2,1,0:T(8,128)S(1)}, f32[2,48,128]{2,1,0:T(8,128)S(1)}, u32[]{:S(2)}, u32[]{:S(2)}) %collective-permute-start.9) | collective-permute-done | bytes 49184 | tf_op jit(solution)/shard_map/ppermute | solution.py:395
  74.5 3.5 %collective-permute-start.10 = (f32[2,48,128]{2,1,0:T(8,128)S(1)}, f32[2,48,128]{2,1,0:T(8,128)S(1)}, u32[]{:S(2)}, u32[]{:S(2)}) collective-permute-start(f32[2,48,128]{2,1,0:T(8,128)S(1)} %pad_maximum_fusion.5), channel_id=1, source_target_pairs={{0,2},{1,3},{2,0},{3,1},{4,6},{5,7},{6,4},{7,5},{8,10},{9,11},{10,... | collective-permute-start | bytes 147464 | tf_op jit(solution)/shard_map/ppermute | solution.py:395
  78.0 1.5 %collective-permute-done.10 = f32[2,48,128]{2,1,0:T(8,128)S(1)} collective-permute-done((f32[2,48,128]{2,1,0:T(8,128)S(1)}, f32[2,48,128]{2,1,0:T(8,128)S(1)}, u32[]{:S(2)}, u32[]{:S(2)}) %collective-permute-start.10) | collective-permute-done | bytes 49184 | tf_op jit(solution)/shard_map/ppermute | solution.py:395
  79.5 4.4 %collective-permute-start.11 = (f32[2,48,128]{2,1,0:T(8,128)S(1)}, f32[2,48,128]{2,1,0:T(8,128)S(1)}, u32[]{:S(2)}, u32[]{:S(2)}) collective-permute-start(f32[2,48,128]{2,1,0:T(8,128)S(1)} %pad_maximum_fusion.6), channel_id=1, source_target_pairs={{0,4},{1,5},{2,6},{3,7},{4,0},{5,1},{6,2},{7,3},{8,12},{9,13},{10,... | collective-permute-start | bytes 147464 | tf_op jit(solution)/shard_map/ppermute | solution.py:395
  84.0 2.5 %collective-permute-done.11 = f32[2,48,128]{2,1,0:T(8,128)S(1)} collective-permute-done((f32[2,48,128]{2,1,0:T(8,128)S(1)}, f32[2,48,128]{2,1,0:T(8,128)S(1)}, u32[]{:S(2)}, u32[]{:S(2)}) %collective-permute-start.11) | collective-permute-done | bytes 49184 | tf_op jit(solution)/shard_map/ppermute | solution.py:395
  86.5 8.4 %collective-permute-start.12 = (f32[2,48,128]{2,1,0:T(8,128)S(1)}, f32[2,48,128]{2,1,0:T(8,128)S(1)}, u32[]{:S(2)}, u32[]{:S(2)}) collective-permute-start(f32[2,48,128]{2,1,0:T(8,128)S(1)} %pad_maximum_fusion.7.mine_ref), channel_id=1, source_target_pairs={{0,8},{1,9},{2,10},{3,11},{4,12},{5,13},{6,14},{7,15},{8,0},{9,1},... | collective-permute-start | bytes 147464 | tf_op jit(solution)/shard_map/ppermute | solution.py:395
  94.9 0.9 collective-permute-done.12.other_ref
  95.8 0.6 copy-done.3
  96.4 15.5 %factor.1 = (f32[128,128]{1,0:T(8,128)}, f32[128,128]{1,0:T(8,128)}, f32[128,128]{1,0:T(8,128)}) custom-call(s32[1]{0:T(128)} %bitcast.core_ref, f32[2,48,128]{2,1,0:T(8,128)} %copy-done.2, f32[2,48,128]{2,1,0:T(8,128)} %copy-done.3), custom_call_target="tpu_custom_call" | custom-call | tf_op jit(solution)/shard_map/factor/pallas_call | solution.py:265
  112.0 8.1 %apply_split.1 = f32[128,4,8,256]{3,2,1,0:T(8,128)} custom-call(f32[128,128]{1,0:T(8,128)} %get-tuple-element.18.w_ref, f32[64,8192]{1,0:T(8,128)} %flatten_modes.1.m_ref, f32[64,8192]{1,0:T(8,128)} %criterion.1.f_ref), custom_call_target="tpu_custom_call" | custom-call | tf_op jit(solution)/shard_map/apply_split/pallas_call | solution.py:370
  (24 shorter events, 0.8 us)
Async XLA Ops:
  6.1 22.4 %collective-permute-start = (f32[64,3,8,256]{3,2,1,0:T(8,128)}, f32[64,3,8,256]{3,2,1,0:T(8,128)S(1)}, u32[]{:S(2)}, u32[]{:S(2)}) collective-permute-start(f32[64,3,8,256]{3,2,1,0:T(8,128)} %get-tuple-element.12), channel_id=1, source_target_pairs={{0,8},{8,16},{16,24},{24,32},{32,40},{40,48},{48,56},{56,64},{64,7... | collective-permute-start | bytes 4718600 | tf_op jit(solution)/shard_map/ppermute | solution.py:387
  8.6 20.5 %collective-permute-start.1 = (f32[64,3,8,256]{3,2,1,0:T(8,128)}, f32[64,3,8,256]{3,2,1,0:T(8,128)S(1)}, u32[]{:S(2)}, u32[]{:S(2)}) collective-permute-start(f32[64,3,8,256]{3,2,1,0:T(8,128)} %get-tuple-element.13), channel_id=1, source_target_pairs={{0,248},{8,0},{16,8},{24,16},{32,24},{40,32},{48,40},{56,48},{64,5... | collective-permute-start | bytes 4718600 | tf_op jit(solution)/shard_map/ppermute | solution.py:387
  9.3 19.2 %collective-permute-start.2 = (f32[2,768,128]{2,1,0:T(8,128)}, f32[2,768,128]{2,1,0:T(8,128)}, u32[]{:S(2)}, u32[]{:S(2)}) collective-permute-start(f32[2,768,128]{2,1,0:T(8,128)} %get-tuple-element.14), channel_id=1, source_target_pairs={{0,1},{1,2},{2,3},{3,4},{4,5},{5,6},{6,7},{7,0},{8,9},{9,10},{10,1... | collective-permute-start | bytes 2359304 | tf_op jit(solution)/shard_map/ppermute | solution.py:387
  10.3 18.2 %collective-permute-start.3 = (f32[2,768,128]{2,1,0:T(8,128)}, f32[2,768,128]{2,1,0:T(8,128)}, u32[]{:S(2)}, u32[]{:S(2)}) collective-permute-start(f32[2,768,128]{2,1,0:T(8,128)} %get-tuple-element.15), channel_id=1, source_target_pairs={{0,7},{1,0},{2,1},{3,2},{4,3},{5,4},{6,5},{7,6},{8,15},{9,8},{10,9... | collective-permute-start | bytes 2359304 | tf_op jit(solution)/shard_map/ppermute | solution.py:387
  28.5 1.2 copy-start
  29.7 1.1 copy-start.1
  49.8 5.6 %collective-permute-start.4 = (f32[2,48,128]{2,1,0:T(8,128)}, f32[2,48,128]{2,1,0:T(8,128)S(1)}, u32[]{:S(2)}, u32[]{:S(2)}) collective-permute-start(f32[2,48,128]{2,1,0:T(8,128)} %get-tuple-element.17), channel_id=1, source_target_pairs={{0,8},{1,9},{2,10},{3,11},{4,12},{5,13},{6,14},{7,15},{8,0},{9,1},... | collective-permute-start | bytes 147464 | tf_op jit(solution)/shard_map/ppermute | solution.py:395
  56.2 3.0 %collective-permute-start.5 = (f32[2,48,128]{2,1,0:T(8,128)S(1)}, f32[2,48,128]{2,1,0:T(8,128)S(1)}, u32[]{:S(2)}, u32[]{:S(2)}) collective-permute-start(f32[2,48,128]{2,1,0:T(8,128)S(1)} %pad_maximum_fusion), channel_id=1, source_target_pairs={{0,16},{1,17},{2,18},{3,19},{4,20},{5,21},{6,22},{7,23},{8,24},{9,... | collective-permute-start | bytes 147464 | tf_op jit(solution)/shard_map/ppermute | solution.py:395
  59.3 4.5 %collective-permute-start.6 = (f32[2,48,128]{2,1,0:T(8,128)S(1)}, f32[2,48,128]{2,1,0:T(8,128)S(1)}, u32[]{:S(2)}, u32[]{:S(2)}) collective-permute-start(f32[2,48,128]{2,1,0:T(8,128)S(1)} %pad_maximum_fusion.1), channel_id=1, source_target_pairs={{0,32},{1,33},{2,34},{3,35},{4,36},{5,37},{6,38},{7,39},{8,40},{9,... | collective-permute-start | bytes 147464 | tf_op jit(solution)/shard_map/ppermute | solution.py:395
  63.8 3.0 %collective-permute-start.7 = (f32[2,48,128]{2,1,0:T(8,128)S(1)}, f32[2,48,128]{2,1,0:T(8,128)S(1)}, u32[]{:S(2)}, u32[]{:S(2)}) collective-permute-start(f32[2,48,128]{2,1,0:T(8,128)S(1)} %pad_maximum_fusion.2), channel_id=1, source_target_pairs={{0,64},{1,65},{2,66},{3,67},{4,68},{5,69},{6,70},{7,71},{8,72},{9,... | collective-permute-start | bytes 147464 | tf_op jit(solution)/shard_map/ppermute | solution.py:395
  66.9 4.5 %collective-permute-start.8 = (f32[2,48,128]{2,1,0:T(8,128)S(1)}, f32[2,48,128]{2,1,0:T(8,128)S(1)}, u32[]{:S(2)}, u32[]{:S(2)}) collective-permute-start(f32[2,48,128]{2,1,0:T(8,128)S(1)} %pad_maximum_fusion.3), channel_id=1, source_target_pairs={{0,128},{1,129},{2,130},{3,131},{4,132},{5,133},{6,134},{7,135},{8... | collective-permute-start | bytes 147464 | tf_op jit(solution)/shard_map/ppermute | solution.py:395
  71.5 3.0 %collective-permute-start.9 = (f32[2,48,128]{2,1,0:T(8,128)S(1)}, f32[2,48,128]{2,1,0:T(8,128)S(1)}, u32[]{:S(2)}, u32[]{:S(2)}) collective-permute-start(f32[2,48,128]{2,1,0:T(8,128)S(1)} %pad_maximum_fusion.4), channel_id=1, source_target_pairs={{0,1},{1,0},{2,3},{3,2},{4,5},{5,4},{6,7},{7,6},{8,9},{9,8},{10,11... | collective-permute-start | bytes 147464 | tf_op jit(solution)/shard_map/ppermute | solution.py:395
  74.5 5.0 %collective-permute-start.10 = (f32[2,48,128]{2,1,0:T(8,128)S(1)}, f32[2,48,128]{2,1,0:T(8,128)S(1)}, u32[]{:S(2)}, u32[]{:S(2)}) collective-permute-start(f32[2,48,128]{2,1,0:T(8,128)S(1)} %pad_maximum_fusion.5), channel_id=1, source_target_pairs={{0,2},{1,3},{2,0},{3,1},{4,6},{5,7},{6,4},{7,5},{8,10},{9,11},{10,... | collective-permute-start | bytes 147464 | tf_op jit(solution)/shard_map/ppermute | solution.py:395
  79.5 7.0 %collective-permute-start.11 = (f32[2,48,128]{2,1,0:T(8,128)S(1)}, f32[2,48,128]{2,1,0:T(8,128)S(1)}, u32[]{:S(2)}, u32[]{:S(2)}) collective-permute-start(f32[2,48,128]{2,1,0:T(8,128)S(1)} %pad_maximum_fusion.6), channel_id=1, source_target_pairs={{0,4},{1,5},{2,6},{3,7},{4,0},{5,1},{6,2},{7,3},{8,12},{9,13},{10,... | collective-permute-start | bytes 147464 | tf_op jit(solution)/shard_map/ppermute | solution.py:395
  86.5 9.3 %copy-start.2 = (f32[2,48,128]{2,1,0:T(8,128)}, f32[2,48,128]{2,1,0:T(8,128)S(1)}, u32[]{:S(2)}) copy-start(f32[2,48,128]{2,1,0:T(8,128)S(1)} %pad_maximum_fusion.7.mine_ref) | copy-start | bytes 147460
  86.5 9.3 %collective-permute-start.12 = (f32[2,48,128]{2,1,0:T(8,128)S(1)}, f32[2,48,128]{2,1,0:T(8,128)S(1)}, u32[]{:S(2)}, u32[]{:S(2)}) collective-permute-start(f32[2,48,128]{2,1,0:T(8,128)S(1)} %pad_maximum_fusion.7.mine_ref), channel_id=1, source_target_pairs={{0,8},{1,9},{2,10},{3,11},{4,12},{5,13},{6,14},{7,15},{8,0},{9,1},... | collective-permute-start | bytes 147464 | tf_op jit(solution)/shard_map/ppermute | solution.py:395
  95.8 0.6 copy-start.3
